TPU v7x, 128 devices: a whole 4x4x4 slice. The times are simulated.
128 devices in a mesh: seq: 16 (over y, x), exp: 8 (over z, core).
Axes of the slice: x: 4, y: 4, z: 4, core: 2. Of those that a mesh axis runs over, the one named last changes fastest.
Arguments:
- queries: bfloat16 [2048, 8192], P('seq', 'exp'), may hold values from -0.5 to 0.5
- keys: bfloat16 [2048, 8192], P('seq', 'exp'), may hold values from -0.5 to 0.5
- values: bfloat16 [2048, 8192], P('seq', 'exp'), may hold values from -6 to 6
- attn_grad: bfloat16 [2048, 8192], P('seq', 'exp'), may hold values from -6 to 6
- log_decay: float32 [2048, 64], P('seq', 'exp'), may hold values from -0.75 to 0, as said below
- moe_grad: bfloat16 [2048, 6144], P('seq', 'exp'), may hold values from -6 to 6
- gate_probs: bfloat16 [2048, 2], P('seq'), may hold values from 0.099609375 to 0.8984375
- expert_ids: int32 [2048, 2], P('seq'), may hold values from 0 to 7, all different within a row; in each aligned block of 128 rows (0 to 127, 128 to 255, ...) at most 48 rows name the same one
- hidden_acts: bfloat16 [8, 768, 9216], P('exp', None, 'seq'), may hold values from -0.3125 to 0.3125
- down_weight: bfloat16 [8, 9216, 6144], P('exp', 'seq'), may hold values from -0.0625 to 0.0625
Outputs:
- query_grad: bfloat16 [2048, 8192], P('seq', 'exp')
- key_grad: bfloat16 [2048, 8192], P('seq', 'exp')
- value_grad: bfloat16 [2048, 8192], P('seq', 'exp')
- hidden_grad: bfloat16 [8, 768, 9216], P('exp', None, 'seq')
- weight_grad: bfloat16 [8, 9216, 6144], P('exp', 'seq')
- gate_grad: float32 [2048, 2], P('seq')
Inputs may be any that keep to these rules, and one draw needn't show every extreme that they name: `expert_ids`: each row names 2 different experts. In the 128 rows of one index of seq no expert is named by more than 48 rows, and every draw has such a block where some expert is named by exactly 48 rows. `log_decay`: log decay of each head at each position; never positive.
All inputs are finite; a program needn't handle non-finite values.
Results may differ from a plain program's by a relative error of at most 0.005.
Values may be sent and summed in bfloat16 or wider, within the bound.
A program may use at most 128 MiB of HBM per device.

v0:
```python
import jax
import jax.numpy as jnp
from jax import lax
from jax.sharding import PartitionSpec as P

precise = lax.Precision.HIGHEST


def prefix(part, axis, combine, identity, reverse):
    count = lax.axis_size(axis)
    place = lax.axis_index(axis)
    ahead = count - 1 - place if reverse else place
    gathered = jax.tree.map(lambda a: lax.all_gather(a, axis), part)
    state = jax.tree.map(lambda a, e: jnp.zeros_like(a) + jnp.asarray(e, a.dtype), part, identity)

    def one(lap, state):
        source = count - 1 - lap if reverse else lap
        return combine(
            state, jax.tree.map(lambda a: lax.dynamic_index_in_dim(a, source, 0, False), gathered)
        )

    return lax.fori_loop(0, ahead, one, state)


def chain_combine(earlier, latter):
    return (jnp.exp(latter[1])[:, None, None] * earlier[0] + latter[0], earlier[1] + latter[1])


def on_device(
    queries,
    keys,
    values,
    attn_grad,
    log_decay,
    moe_grad,
    gate_probs,
    expert_ids,
    hidden_acts,
    down_weight,
):
    tok_count = queries.shape[0]
    head_count = log_decay.shape[1]
    head_width = queries.shape[1] // head_count
    shaped = (tok_count, head_count, head_width)
    query_f = queries.astype(jnp.float32).reshape(shaped)
    key_f = keys.astype(jnp.float32).reshape(shaped)
    value_f = values.astype(jnp.float32).reshape(shaped)
    grad_f = attn_grad.astype(jnp.float32).reshape(shaped)
    cumul = jnp.cumsum(log_decay, axis=0)
    total = cumul[-1]
    tail_w = jnp.exp(total[None, :] - cumul)
    lead_w = jnp.exp(cumul)
    state_kv = jnp.einsum("th,thi,thj->hij", tail_w, key_f, value_f, precision=precise)
    state_qg = jnp.einsum("th,thi,thj->hij", lead_w, query_f, grad_f, precision=precise)
    zero_state = jnp.zeros_like(state_kv)
    zero_gain = jnp.zeros_like(total)
    incoming = prefix((state_kv, total), "seq", chain_combine, (zero_state, zero_gain), False)[0]
    upcoming = prefix((state_qg, total), "seq", chain_combine, (zero_state, zero_gain), True)[0]
    causal = jnp.arange(tok_count)[:, None] >= jnp.arange(tok_count)[None, :]
    spread = cumul.T[:, :, None] - cumul.T[:, None, :]
    decay_mask = jnp.exp(jnp.where(causal[None], spread, -jnp.inf))
    grad_scores = jnp.einsum("thj,shj->hts", grad_f, value_f, precision=precise) * decay_mask
    qk_scores = jnp.einsum("thi,shi->hts", query_f, key_f, precision=precise) * decay_mask
    query_g = jnp.einsum("hts,shi->thi", grad_scores, key_f, precision=precise)
    query_g = query_g + lead_w[:, :, None] * jnp.einsum(
        "thj,hij->thi", grad_f, incoming, precision=precise
    )
    key_g = jnp.einsum("hts,thi->shi", grad_scores, query_f, precision=precise)
    key_g = key_g + tail_w[:, :, None] * jnp.einsum(
        "shj,hij->shi", value_f, upcoming, precision=precise
    )
    value_g = jnp.einsum("hts,thj->shj", qk_scores, grad_f, precision=precise)
    value_g = value_g + tail_w[:, :, None] * jnp.einsum(
        "shi,hij->shj", key_f, upcoming, precision=precise
    )
    flat_width = head_count * head_width
    query_grad = query_g.reshape(tok_count, flat_width).astype(jnp.bfloat16)
    key_grad = key_g.reshape(tok_count, flat_width).astype(jnp.bfloat16)
    value_grad = value_g.reshape(tok_count, flat_width).astype(jnp.bfloat16)
    expert_here = lax.axis_index("exp")
    cap_size = hidden_acts.shape[1] // lax.axis_size("seq")
    chosen_here = expert_ids == expert_here
    routed = jnp.any(chosen_here, axis=1)
    token_gate = jnp.sum(jnp.where(chosen_here, gate_probs.astype(jnp.float32), 0.0), axis=1)
    slot_rank = jnp.cumsum(routed.astype(jnp.int32)) - 1
    slot_ids = jnp.arange(cap_size, dtype=jnp.int32)
    selector = ((slot_rank[None, :] == slot_ids[:, None]) & routed[None, :]).astype(jnp.float32)
    slot_gate = jnp.dot(selector, token_gate, precision=precise).astype(jnp.bfloat16)
    whole_rows = lax.all_gather(moe_grad, "exp", axis=1, tiled=True)
    slot_rows = jnp.dot(
        selector.astype(jnp.bfloat16), whole_rows, preferred_element_type=jnp.float32
    ).astype(jnp.bfloat16)
    weight_here = down_weight[0]
    hidden_here = hidden_acts[0]
    piece_rows = lax.all_gather(slot_rows, "seq", axis=0, tiled=True)
    piece_gate = lax.all_gather(slot_gate, "seq", axis=0, tiled=True)
    back_rows = lax.dot_general(
        piece_rows, weight_here, (((1,), (1,)), ((), ())), preferred_element_type=jnp.float32
    )
    gate_col = piece_gate.astype(jnp.float32)[:, None]
    hidden_out = (gate_col * back_rows).astype(jnp.bfloat16)
    piece_parts = jnp.sum(back_rows * hidden_here.astype(jnp.float32), axis=1)
    slot_parts = piece_parts
    weighted = (gate_col * piece_rows.astype(jnp.float32)).astype(jnp.bfloat16)
    grad_sum = lax.dot_general(
        hidden_here, weighted, (((0,), (0,)), ((), ())), preferred_element_type=jnp.float32
    )
    grad_sum, hidden_out, slot_parts = (grad_sum, hidden_out, slot_parts)
    own_parts = lax.psum_scatter(slot_parts, "seq", scatter_dimension=0, tiled=True)
    per_token = jnp.dot(selector.T, own_parts, precision=precise)
    local_gate = jnp.where(chosen_here, per_token[:, None], 0.0)
    gate_grad = lax.psum(local_gate, "exp")
    return (
        query_grad,
        key_grad,
        value_grad,
        hidden_out[None],
        grad_sum.astype(jnp.bfloat16)[None],
        gate_grad,
    )


def solution(mesh):
    return jax.shard_map(
        on_device,
        mesh=mesh,
        in_specs=(
            P("seq", "exp"),
            P("seq", "exp"),
            P("seq", "exp"),
            P("seq", "exp"),
            P("seq", "exp"),
            P("seq", "exp"),
            P("seq", None),
            P("seq", None),
            P("exp", None, "seq"),
            P("exp", "seq", None),
        ),
        out_specs=(
            P("seq", "exp"),
            P("seq", "exp"),
            P("seq", "exp"),
            P("exp", None, "seq"),
            P("exp", "seq", None),
            P("seq", None),
        ),
        check_vma=False,
    )
```

profile of v0, /device:TPU:1, one launch (start us, length us, event | category | flops | bytes accessed | tf_op | source)
XLA Modules:
  0.0 343.7 jit_solution(9725436786065418335)
XLA Ops:
  10.2 1.2 fusion.21
  13.8 1.5 fusion.18
  16.5 21.5 %all-gather.8.cloned.1.call-done = bf16[128,6144]{1,0:T(8,128)(2,1)} async-done(((bf16[128,768]{1,0:T(8,128)(2,1)}), bf16[128,6144]{1,0:T(8,128)(2,1)}) %all-gather.8.cloned.1.call-update) | async-done | bytes 1572880 | tf_op jit(solution)/shard_map/all_gather | solution.py:89
  37.9 2.6 convolution_convert_fusion
  42.1 33.4 %all-reduce = bf16[768]{0:T(1024)(128)(2,1)S(1)} all-reduce(bf16[768]{0:T(1024)(128)(2,1)S(1)} %dynamic-update-slice), channel_id=1, replica_groups=mesh['seq'=16,'exp'=8] {'seq'}, use_global_device_ids=true, to_apply=%add | all-reduce | flops 768 | bytes 3072
  76.2 15.0 %all-gather.2 = f32[16,1,8]{2,1,0:T(1,128)S(1)} all-gather(f32[1,1,8]{2,1,0:T(1,128)S(1)} %get-tuple-element.211), channel_id=1, replica_groups=mesh['seq'=16,'exp'=8] {'seq'}, dimensions={0}, use_global_device_ids=true | all-gather | bytes 544 | tf_op jit(solution)/shard_map/all_gather | solution.py:13
  91.9 19.4 %all-gather.12.cloned.1.call-done = f32[128,128,128]{2,1,0:T(8,128)} async-done(((f32[8,128,128]{2,1,0:T(8,128)}), f32[128,128,128]{2,1,0:T(8,128)}) %all-gather.12.cloned.1.call-update) | async-done | bytes 8388624 | tf_op jit(solution)/shard_map/all_gather | solution.py:13
  113.2 70.5 %all-gather.14.cloned.1.call-done = f32[128,128,128]{2,1,0:T(8,128)} async-done(((f32[8,128,128]{2,1,0:T(8,128)}), f32[128,128,128]{2,1,0:T(8,128)}) %all-gather.14.cloned.1.call-update) | async-done | bytes 8388624 | tf_op jit(solution)/shard_map/all_gather | solution.py:13
  183.7 18.6 %while.27 = (s32[]{:T(128)}, f32[8,128,128]{2,1,0:T(8,128)S(1)}, s32[]{:T(128)}, f32[16,8]{1,0:T(8,128)S(1)}, f32[16,8,128,128]{3,2,1,0:T(8,128)}, /*index=5*/s32[]{:T(128)}, s32[]{:T(128)}, s32[]{:T(128)}, s32[]{:T(128)}) while((s32[]{:T(128)}, f32[8,128,128]{2,1,0:T(8,128)S(1)}, s32[]{:T(128)}, f32[16,8]{1,0:T(8,128)S(1)}, ...), condition=%wide.region_4.5_spmd, body=%wide.region_3.4_spmd.sunk | while | flops 262150 | bytes 1573115 | solution.py:22
  183.8 1.2 bitcast_add_fusion.5
  185.0 1.2 bitcast_add_fusion.5
  186.2 1.2 bitcast_add_fusion.5
  187.5 1.2 bitcast_add_fusion.5
  188.7 1.2 bitcast_add_fusion.5
  189.9 1.2 bitcast_add_fusion.5
  191.2 1.2 bitcast_add_fusion.5
  194.9 1.2 bitcast_add_fusion.5
  196.1 1.2 bitcast_add_fusion.5
  197.4 1.2 bitcast_add_fusion.5
  206.1 55.5 %all-gather.10.cloned.1.call-done = bf16[768,6144]{1,0:T(8,128)(2,1)} async-done(((bf16[48,6144]{1,0:T(8,128)(2,1)}), bf16[768,6144]{1,0:T(8,128)(2,1)}) %all-gather.10.cloned.1.call-update) | async-done | bytes 9437200 | tf_op jit(solution)/shard_map/all_gather | solution.py:95
  261.6 11.6 %multiply_reduce_fusion = (f32[768]{0:T(1024)S(1)}, bf16[1,768,576]{1,2,0:T(8,128)(2,1)}) fusion(bf16[1,768,576]{1,2,0:T(8,128)(2,1)} %param.22, f32[768]{0:T(1024)S(1)} %convert_element_type.83, bf16[768,6144]{1,0:T(8,128)(2,1)} %all-gather.10.cloned.1.call-done, bf16[1,576,6144]{2,1,0:T(8,128)(2,1)} %param.23), kind=kOutput, calls=%fused_computation.12 | convolution fusion | flops 5438028800 | bytes 18290688 | tf_op jit(solution)/shard_map/dot_general | solution.py:97
  273.2 31.2 %all-reduce.1 = f32[768]{0:T(1024)S(1)} all-reduce(f32[768]{0:T(1024)S(1)} %get-tuple-element.206), channel_id=4, replica_groups=mesh['seq'=16,'exp'=8] {'seq'}, use_global_device_ids=true, to_apply=%region_9.10.clone | all-reduce | flops 768 | bytes 6144
  304.5 20.6 %psum.7 = f32[128,2]{0,1:T(2,128)} all-reduce(f32[128,2]{0,1:T(2,128)S(1)} %broadcast_select_fusion), channel_id=1, replica_groups=mesh['seq'=16,'exp'=8] {'exp'}, use_global_device_ids=true, to_apply=%region_10.11 | all-reduce | flops 256 | bytes 2048 | tf_op jit(solution)/shard_map/psum | solution.py:112
  325.1 12.0 %fusion.3 = bf16[1,576,6144]{2,1,0:T(8,128)(2,1)} fusion(bf16[768,6144]{1,0:T(8,128)(2,1)} %all-gather.10.cloned.1.call-done, f32[768]{0:T(1024)S(1)} %convert_element_type.83, bf16[1,768,576]{1,2,0:T(8,128)(2,1)S(1)} %copy-done.2), kind=kOutput, calls=%fused_computation.8 | convolution fusion | flops 5453512704 | bytes 17402880 | tf_op jit(solution)/shard_map/dot_general | solution.py:105
  (72 shorter events, 20.3 us)
Async XLA Ops:
  7.2 3.0 copy-start
  7.2 33.4 %copy-start.1 = (u32[128]{0:T(128)S(1)}, u32[128]{0:T(128)}, u32[]{:S(2)}) copy-start(u32[128]{0:T(128)} %constant.81) | copy-start | bytes 1540
  7.2 30.7 %all-gather.8.cloned.1.call-start = ((), (), s32[]{:S(2)}) async-start(), calls=%async_computation | async-start | bytes 1769472 | tf_op jit(solution)/shard_map/all_gather | solution.py:89
  7.9 103.3 %all-gather.12.cloned.1.call-start = ((), (), s32[]{:S(2)}) async-start(), calls=%async_computation.2 | async-start | bytes 8912896 | tf_op jit(solution)/shard_map/all_gather | solution.py:13
  11.4 172.3 %all-gather.14.cloned.1.call-start = ((), (), s32[]{:S(2)}) async-start(), calls=%async_computation.3 | async-start | bytes 8912896 | tf_op jit(solution)/shard_map/all_gather | solution.py:13
  15.3 246.3 %all-gather.10.cloned.1.call-start = ((), (), s32[]{:S(2)}) async-start(), calls=%async_computation.1 | async-start | bytes 10027008 | tf_op jit(solution)/shard_map/all_gather | solution.py:95
  206.1 119.0 %copy-start.2 = (bf16[1,768,576]{1,2,0:T(8,128)(2,1)S(1)}, bf16[1,768,576]{1,2,0:T(8,128)(2,1)}, u32[]{:S(2)}) copy-start(bf16[1,768,576]{1,2,0:T(8,128)(2,1)} %param.22) | copy-start | bytes 2654212
Sparse Core Ops, SparseCore 0:
  9.7 28.1 all-gather.7
  40.6 70.5 all-gather.11
  113.4 70.2 all-gather.13
  186.2 75.2 all-gather.9
where the time goes:
time: 345 us; the launch traced here: 344 us
  waiting for transfers between devices  168 us (49%)
  blocking collectives  100 us (29%)
  matrix products  33 us (10%)
  other arithmetic  19.2 us (6%)
  between operations  15.2 us (4%)
  local copies, waits for them, and re-layouts  8.11 us (2%)
    all_gather x2, waiting for transfers between devices, prefix(): gathered = jax.tree.map(lambda a: lax.all_gather(a, axis), part)  89.8 us
    unnamed x2, blocking collectives  64.5 us
    all_gather x1, waiting for transfers between devices, on_device(): piece_rows = lax.all_gather(slot_rows, 'seq', axis=0, tiled=True)  55.5 us
    all_gather x1, waiting for transfers between devices, on_device(): whole_rows = lax.all_gather(moe_grad, 'exp', axis=1, tiled=True)  21.5 us
    psum x1, blocking collectives, on_device(): gate_grad = lax.psum(local_gate, 'exp')  20.6 us
    add x15, other arithmetic, chain_combine(): jnp.exp(latter[1])[:, None, None] * earlier[0] + latter[0]  17.9 us
    all_gather x1, blocking collectives, prefix(): gathered = jax.tree.map(lambda a: lax.all_gather(a, axis), part)  15 us
    dot_general x1, matrix products, on_device(): lax.dot_general(hidden_here, weighted, (((0,), (0,)), ((), ())), preferre...  12 us
  transfers between devices with their start and end apart: 4, of which 4 were waited for; matrix products, arithmetic and copies ran while one was open for 11% of the time, Pallas kernels for 0%

commit v1 on v0

--- a/solution.py
+++ b/solution.py
@@ -2,6 +2,7 @@
 import jax.numpy as jnp
 from jax import lax
 from jax.sharding import PartitionSpec as P
+from jax.lax import all_to_all, psum
 
 precise = lax.Precision.HIGHEST
 
@@ -86,7 +87,16 @@
     slot_ids = jnp.arange(cap_size, dtype=jnp.int32)
     selector = ((slot_rank[None, :] == slot_ids[:, None]) & routed[None, :]).astype(jnp.float32)
     slot_gate = jnp.dot(selector, token_gate, precision=precise).astype(jnp.bfloat16)
-    whole_rows = lax.all_gather(moe_grad, "exp", axis=1, tiled=True)
+    list_the_strings = lambda xx, which_dim: jnp.concatenate(
+        all_to_all(
+            jnp.stack([xx for _ in range(psum(1, axis_name="exp"))], 0),
+            split_axis=0,
+            axis_name="exp",
+            concat_axis=0,
+        ),
+        which_dim,
+    )
+    whole_rows = list_the_strings(moe_grad, 1)
     slot_rows = jnp.dot(
         selector.astype(jnp.bfloat16), whole_rows, preferred_element_type=jnp.float32
     ).astype(jnp.bfloat16)

time: 345 us -> 319 us (0.925)
  waiting for transfers between devices: 168 us -> 135 us
  starting transfers between devices: 0.16 us -> 6.9 us
    all_gather x2, waiting for transfers between devices: 89.8 us -> 59.6 us  [prefix(): gathered = jax.tree.map(lambda a: lax.all_gather(a, axis), part)]
    all_gather x1 -> x0, waiting for transfers between devices: 21.5 us -> none  [on_device(): whole_rows = lax.all_gather(moe_grad, 'exp', axis=1, tiled=True)]
    all_to_all x0 -> x1, waiting for transfers between devices: none -> 20.3 us  [on_device(): all_to_all(jnp.stack([xx for _ in range(psum(1, axis_name='exp'))], 0), s...]
    all_to_all x0 -> x1, starting transfers between devices: none -> 6.81 us  [on_device(): all_to_all(jnp.stack([xx for _ in range(psum(1, axis_name='exp'))], 0), s...]
    unnamed x15 -> x20, local copies, waits for them, and re-layouts: 6.47 us -> 7.59 us
  transfers between devices with their start and end apart: 4 -> 4, of which waited for: 4 -> 3; matrix products, arithmetic and copies ran while one was open for 11% -> 11% of each run, Pallas kernels for 0% -> 0%
where the time goes in v1:
time: 319 us; the launch traced here: 318 us
  waiting for transfers between devices  135 us (42%)
  blocking collectives  98.9 us (31%)
  matrix products  31.8 us (10%)
  other arithmetic  18.5 us (6%)
  between operations  15.3 us (5%)
  local copies, waits for them, and re-layouts  10.6 us (3%)
  starting transfers between devices  6.9 us (2%)
    unnamed x2, blocking collectives  65.4 us
    all_gather x2, waiting for transfers between devices, prefix(): gathered = jax.tree.map(lambda a: lax.all_gather(a, axis), part)  59.6 us
    all_gather x1, waiting for transfers between devices, on_device(): piece_rows = lax.all_gather(slot_rows, 'seq', axis=0, tiled=True)  55.6 us
    psum x1, blocking collectives, on_device(): gate_grad = lax.psum(local_gate, 'exp')  20.6 us
    all_to_all x1, waiting for transfers between devices, on_device(): all_to_all(jnp.stack([xx for _ in range(psum(1, axis_name='exp'))], 0), s...  20.3 us
    add x15, other arithmetic, chain_combine(): jnp.exp(latter[1])[:, None, None] * earlier[0] + latter[0]  18 us
    all_gather x1, blocking collectives, prefix(): gathered = jax.tree.map(lambda a: lax.all_gather(a, axis), part)  13 us
    dot_general x1, matrix products, on_device(): lax.dot_general(hidden_here, weighted, (((0,), (0,)), ((), ())), preferre...  11.9 us
  transfers between devices with their start and end apart: 4, of which 3 were waited for; matrix products, arithmetic and copies ran while one was open for 11% of the time, Pallas kernels for 0%

profile of v1, /device:TPU:1, one launch (start us, length us, event | category | flops | bytes accessed | tf_op | source)
XLA Modules:
  0.0 317.9 jit_solution(10792344098132005387)
XLA Ops:
  9.5 1.2 fusion.21
  13.1 1.5 fusion.18
  15.7 1.4 stack.2
  17.0 6.8 %all-to-all-start = ((bf16[8,128,768]{1,2,0:T(8,128)(2,1)}), bf16[8,128,768]{1,2,0:T(8,128)(2,1)S(1)}, u32[]{:S(2)}, u32[]{:S(2)}) async-start(bf16[8,128,768]{1,2,0:T(8,128)(2,1)} %stack.2), calls=%async_computation | async-start | bytes 3145728 | tf_op jit(solution)/shard_map/all_to_all | solution.py:91
  24.3 20.3 %all-to-all-done = bf16[8,128,768]{1,2,0:T(8,128)(2,1)S(1)} async-done(((bf16[8,128,768]{1,2,0:T(8,128)(2,1)}), bf16[8,128,768]{1,2,0:T(8,128)(2,1)S(1)}, u32[]{:S(2)}, u32[]{:S(2)}) %all-to-all-start) | async-done | bytes 1572896 | tf_op jit(solution)/shard_map/all_to_all | solution.py:91
  44.5 1.5 convolution_convert_fusion
  47.7 34.2 %all-reduce = bf16[768]{0:T(1024)(128)(2,1)S(1)} all-reduce(bf16[768]{0:T(1024)(128)(2,1)S(1)} %dynamic-update-slice), channel_id=1, replica_groups=mesh['seq'=16,'exp'=8] {'seq'}, use_global_device_ids=true, to_apply=%add | all-reduce | flops 768 | bytes 3072
  82.6 13.0 %all-gather.2 = f32[16,1,8]{2,1,0:T(1,128)S(1)} all-gather(f32[1,1,8]{2,1,0:T(1,128)S(1)} %get-tuple-element.211), channel_id=1, replica_groups=mesh['seq'=16,'exp'=8] {'seq'}, dimensions={0}, use_global_device_ids=true | all-gather | bytes 544 | tf_op jit(solution)/shard_map/all_gather | solution.py:14
  98.3 59.5 %all-gather.11.cloned.1.call-done = f32[128,128,128]{2,1,0:T(8,128)} async-done(((f32[8,128,128]{2,1,0:T(8,128)}), f32[128,128,128]{2,1,0:T(8,128)}) %all-gather.11.cloned.1.call-update) | async-done | bytes 8388624 | tf_op jit(solution)/shard_map/all_gather | solution.py:14
  157.9 18.6 %while.27 = (s32[]{:T(128)}, f32[8,128,128]{2,1,0:T(8,128)S(1)}, s32[]{:T(128)}, f32[16,8]{1,0:T(8,128)S(1)}, f32[16,8,128,128]{3,2,1,0:T(8,128)}, /*index=5*/s32[]{:T(128)}, s32[]{:T(128)}, s32[]{:T(128)}, s32[]{:T(128)}) while((s32[]{:T(128)}, f32[8,128,128]{2,1,0:T(8,128)S(1)}, s32[]{:T(128)}, f32[16,8]{1,0:T(8,128)S(1)}, ...), condition=%wide.region_4.5_spmd, body=%wide.region_3.4_spmd.sunk | while | flops 262150 | bytes 1573115 | solution.py:23
  157.9 1.2 bitcast_add_fusion.5
  161.6 1.2 bitcast_add_fusion.5
  162.8 1.2 bitcast_add_fusion.5
  164.1 1.2 bitcast_add_fusion.5
  169.0 1.2 bitcast_add_fusion.5
  170.3 1.2 bitcast_add_fusion.5
  171.5 1.2 bitcast_add_fusion.5
  174.0 1.2 bitcast_add_fusion.5
  175.3 1.2 bitcast_add_fusion.5
  180.3 55.6 %all-gather.7.cloned.1.call-done = bf16[768,6144]{1,0:T(8,128)(2,1)} async-done(((bf16[48,6144]{1,0:T(8,128)(2,1)}), bf16[768,6144]{1,0:T(8,128)(2,1)}) %all-gather.7.cloned.1.call-update) | async-done | bytes 9437200 | tf_op jit(solution)/shard_map/all_gather | solution.py:105
  235.9 11.6 %multiply_reduce_fusion = (f32[768]{0:T(1024)S(1)}, bf16[1,768,576]{1,2,0:T(8,128)(2,1)}) fusion(bf16[1,768,576]{1,2,0:T(8,128)(2,1)} %param.22, f32[768]{0:T(1024)S(1)} %convert_element_type.83, bf16[768,6144]{1,0:T(8,128)(2,1)} %all-gather.7.cloned.1.call-done, bf16[1,576,6144]{2,1,0:T(8,128)(2,1)} %param.23), kind=kOutput, calls=%fused_computation.12 | convolution fusion | flops 5438028800 | bytes 18290688 | tf_op jit(solution)/shard_map/dot_general | solution.py:107
  247.5 31.2 %all-reduce.1 = f32[768]{0:T(1024)S(1)} all-reduce(f32[768]{0:T(1024)S(1)} %get-tuple-element.206), channel_id=4, replica_groups=mesh['seq'=16,'exp'=8] {'seq'}, use_global_device_ids=true, to_apply=%region_9.10.clone | all-reduce | flops 768 | bytes 6144
  278.9 20.6 %psum.7 = f32[128,2]{0,1:T(2,128)} all-reduce(f32[128,2]{0,1:T(2,128)S(1)} %broadcast_select_fusion), channel_id=1, replica_groups=mesh['seq'=16,'exp'=8] {'exp'}, use_global_device_ids=true, to_apply=%region_10.11 | all-reduce | flops 256 | bytes 2048 | tf_op jit(solution)/shard_map/psum | solution.py:122
  299.4 11.9 %fusion.3 = bf16[1,576,6144]{2,1,0:T(8,128)(2,1)} fusion(bf16[768,6144]{1,0:T(8,128)(2,1)} %all-gather.7.cloned.1.call-done, f32[768]{0:T(1024)S(1)} %convert_element_type.83, bf16[1,768,576]{1,2,0:T(8,128)(2,1)S(1)} %copy-done.4), kind=kOutput, calls=%fused_computation.8 | convolution fusion | flops 5453512704 | bytes 17402880 | tf_op jit(solution)/shard_map/dot_general | solution.py:115
  (77 shorter events, 21.2 us)
Async XLA Ops:
  7.2 2.3 copy-start
  7.2 38.9 %copy-start.1 = (u32[128]{0:T(128)S(1)}, u32[128]{0:T(128)}, u32[]{:S(2)}) copy-start(u32[128]{0:T(128)} %constant.81) | copy-start | bytes 1540
  7.2 16.6 %copy-start.3 = (bf16[128,2]{0,1:T(2,128)(2,1)S(1)}, bf16[128,2]{0,1:T(2,128)(2,1)}, u32[]{:S(2)}) copy-start(bf16[128,2]{0,1:T(2,128)(2,1)} %param.20) | copy-start | bytes 1540
  7.2 16.6 %copy-start.2 = (s32[128,2]{0,1:T(2,128)S(1)}, s32[128,2]{0,1:T(2,128)}, u32[]{:S(2)}) copy-start(s32[128,2]{0,1:T(2,128)} %param.21) | copy-start | bytes 3076
  7.2 89.1 %all-gather.9.cloned.1.call-start = ((), (), s32[]{:S(2)}) async-start(), calls=%async_computation.2 | async-start | bytes 8912896 | tf_op jit(solution)/shard_map/all_gather | solution.py:14
  10.7 147.1 %all-gather.11.cloned.1.call-start = ((), (), s32[]{:S(2)}) async-start(), calls=%async_computation.3 | async-start | bytes 8912896 | tf_op jit(solution)/shard_map/all_gather | solution.py:14
  17.0 27.5 %all-to-all-start = ((bf16[8,128,768]{1,2,0:T(8,128)(2,1)}), bf16[8,128,768]{1,2,0:T(8,128)(2,1)S(1)}, u32[]{:S(2)}, u32[]{:S(2)}) async-start(bf16[8,128,768]{1,2,0:T(8,128)(2,1)} %stack.2), calls=%async_computation | async-start | bytes 3145728 | tf_op jit(solution)/shard_map/all_to_all | solution.py:91
  23.8 212.0 %all-gather.7.cloned.1.call-start = ((), (), s32[]{:S(2)}) async-start(), calls=%async_computation.1 | async-start | bytes 10027008 | tf_op jit(solution)/shard_map/all_gather | solution.py:105
  180.3 119.1 %copy-start.4 = (bf16[1,768,576]{1,2,0:T(8,128)(2,1)S(1)}, bf16[1,768,576]{1,2,0:T(8,128)(2,1)}, u32[]{:S(2)}) copy-start(bf16[1,768,576]{1,2,0:T(8,128)(2,1)} %param.22) | copy-start | bytes 2654212
Sparse Core Ops, SparseCore 0:
  10.8 74.4 all-gather.8
  87.5 70.2 all-gather.10
  160.5 75.2 all-gather.6
